TPU v7x, 128 devices: a whole 4x4x4 slice. The times are simulated.
128 devices in a mesh: req: 32 (over x, y, core), mlp: 4 (over z).
Axes of the slice: x: 4, y: 4, z: 4, core: 2. Of those that a mesh axis runs over, the one named last changes fastest.
Arguments:
- hidden_in: bfloat16 [64, 512, 2048], P('req'), may hold values from -6 to 6
- lengths: int32 [64], replicated, may hold values from 1 to 512, 16384 in all
- slot_request: int32 [64], replicated, may hold values from 0 to 63, each once
- adapter_of: int32 [64], replicated, may hold values from 0 to 63, as said below
- adapter_slot: int32 [64], replicated, may hold values from 0 to 63, each once
- norm_gain_attn: float32 [2048], replicated, may hold values from 0.5 to 1.5
- norm_gain_mlp: float32 [2048], replicated, may hold values from 0.5 to 1.5
- final_gain: float32 [2048], replicated, may hold values from 0.5 to 1.5
- w_qkv: bfloat16 [2048, 3, 2048], P(None, None, 'mlp')
- w_out: bfloat16 [2048, 2048], P('mlp'), may hold values from -0.125 to 0.125
- w_gateup: bfloat16 [2048, 2, 4096], P('req', None, 'mlp'), may hold values from -0.125 to 0.125
- w_down: bfloat16 [4096, 2048], P('mlp', 'req'), may hold values from -0.09375 to 0.09375
- adapter_down: bfloat16 [64, 16, 2048], P('req'), may hold values from -0.125 to 0.125
- adapter_up: bfloat16 [64, 16, 2048], P('req', None, 'mlp'), may hold values from -1.5 to 1.5
- vocab: bfloat16 [49152, 2048], P(('req', 'mlp')), may hold values from -0.375 to 0.375
Outputs:
- out_hidden: bfloat16 [64, 512, 2048], P('req')
- request_norm: float32 [64], replicated
- request_peak: float32 [64], replicated
Inputs may be any that keep to these rules, and one draw needn't show every extreme that they name: Some request has exactly 512 tokens, and all lengths together sum to 16384. `slot_request`: each request sits in exactly one slot. `adapter_of`: exactly 16 distinct adapters are named. `adapter_slot`: each adapter sits in exactly one row of the adapter tables.
All inputs are finite; a program needn't handle non-finite values.
Results may differ from a plain program's by a relative error of at most 0.018.
Values may be sent and summed in bfloat16 or wider, within the bound.
A program may use at most 128 MiB of HBM per device.

v0:
```python
import jax
import jax.numpy as jnp
from jax import lax
from jax.sharding import PartitionSpec as P

HEAD_WIDTH = 64
EPSILON = 1e-05
ROPE_BASE = 130000.0
ADAPTER_SCALE = 2.0
MASKED = -1e30


def rms_norm(values, gain):
    return values * lax.rsqrt(jnp.mean(values * values, axis=-1, keepdims=True) + EPSILON) * gain


def rotary_embedded(tensor):
    length = tensor.shape[-3]
    half_width = tensor.shape[-1] // 2
    frequency = ROPE_BASE ** (-(jnp.arange(half_width, dtype=jnp.float32) * 2.0 / tensor.shape[-1]))
    angles = jnp.arange(length, dtype=jnp.float32)[:, None] * frequency[None, :]
    cosine = jnp.cos(angles)[:, None, :]
    sine_part = jnp.sin(angles)[:, None, :]
    front_half = tensor[..., :half_width]
    back_half = tensor[..., half_width:]
    return jnp.concatenate(
        [front_half * cosine - back_half * sine_part, back_half * cosine + front_half * sine_part],
        axis=-1,
    )


def per_device(
    hidden_in,
    lengths,
    slot_request,
    adapter_of,
    adapter_slot,
    norm_gain_attn,
    norm_gain_mlp,
    final_gain,
    w_qkv,
    w_out,
    w_gateup,
    w_down,
    adapter_down,
    adapter_up,
    vocab,
):
    req_index = lax.axis_index("req")
    slots_number, sequence_length, width = hidden_in.shape
    row_count = slots_number * sequence_length
    head_cols = w_qkv.shape[2]
    heads_number = head_cols // HEAD_WIDTH
    unit_cols = w_gateup.shape[2]
    requests = lax.dynamic_slice_in_dim(slot_request, req_index * slots_number, slots_number)
    own_lengths = jnp.take(lengths, requests)
    own_adapters = jnp.take(adapter_of, requests)
    table_rows = jnp.take(adapter_slot, own_adapters)
    positions = jnp.arange(sequence_length, dtype=jnp.int32)
    residual_in = hidden_in.astype(jnp.float32)
    normed = rms_norm(residual_in, norm_gain_attn).astype(jnp.bfloat16)
    projected_rows = jnp.dot(
        normed.reshape(row_count, width),
        w_qkv.reshape(width, 3 * head_cols),
        preferred_element_type=jnp.float32,
    ).reshape(slots_number, sequence_length, 3, head_cols)
    down_all, up_all = (
        lax.all_gather(adapter_down, "req", axis=0, tiled=True),
        lax.all_gather(adapter_up, "req", axis=0, tiled=True),
    )
    down_rows = jnp.take(down_all, table_rows, axis=0)
    up_rows = jnp.take(up_all, table_rows, axis=0)
    low_rank = jnp.einsum(
        "bsd,brd->bsr", normed, down_rows, preferred_element_type=jnp.float32
    ).astype(jnp.bfloat16)
    raised_rows = jnp.einsum("bsr,brc->bsc", low_rank, up_rows, preferred_element_type=jnp.float32)
    queries = rotary_embedded(
        (projected_rows[:, :, 0] + ADAPTER_SCALE * raised_rows).reshape(
            slots_number, sequence_length, heads_number, HEAD_WIDTH
        )
    ).astype(jnp.bfloat16)
    key_heads = rotary_embedded(
        projected_rows[:, :, 1].reshape(slots_number, sequence_length, heads_number, HEAD_WIDTH)
    ).astype(jnp.bfloat16)
    value_heads = (
        projected_rows[:, :, 2]
        .reshape(slots_number, sequence_length, heads_number, HEAD_WIDTH)
        .astype(jnp.bfloat16)
    )
    causal = positions[None, :] <= positions[:, None]

    def attend(slot_items):
        query_one, key_one, value_one, length = slot_items
        scores = jnp.einsum(
            "qhd,khd->hqk", query_one, key_one, preferred_element_type=jnp.float32
        ) * HEAD_WIDTH ** (-0.5)
        allowed = causal & (positions[None, :] < length)
        scores = jnp.where(allowed[None], scores, MASKED)
        probabilities = jax.nn.softmax(scores, axis=-1).astype(jnp.bfloat16)
        return jnp.einsum(
            "hqk,khd->qhd", probabilities, value_one, preferred_element_type=jnp.float32
        ).astype(jnp.bfloat16)

    attended = lax.map(attend, (queries, key_heads, value_heads, own_lengths))
    head_part = jnp.dot(
        attended.reshape(row_count, head_cols), w_out, preferred_element_type=jnp.float32
    )
    mixed_heads = lax.psum(head_part.astype(jnp.bfloat16), "mlp").astype(jnp.float32)
    stream = (residual_in + mixed_heads.reshape(slots_number, sequence_length, width)).astype(
        jnp.bfloat16
    )
    normed_mid = (
        rms_norm(stream.astype(jnp.float32), norm_gain_mlp)
        .astype(jnp.bfloat16)
        .reshape(row_count, width)
    )
    shard_piece = lax.all_gather(w_gateup, "req", axis=0, tiled=True)
    gate_up = jnp.dot(
        normed_mid,
        shard_piece.reshape(shard_piece.shape[0], 2 * unit_cols),
        preferred_element_type=jnp.float32,
    )
    activated = (jax.nn.silu(gate_up[:, :unit_cols]) * gate_up[:, unit_cols:]).astype(jnp.bfloat16)
    unit_part = jnp.dot(
        activated,
        lax.all_gather(w_down, "req", axis=1, tiled=True),
        preferred_element_type=jnp.float32,
    )
    unit_total = lax.psum(unit_part.astype(jnp.bfloat16), "mlp").astype(jnp.float32)
    result = stream.astype(jnp.float32) + unit_total.reshape(slots_number, sequence_length, width)
    live = positions[None, :] < own_lengths[:, None]
    out_hidden = jnp.where(live[:, :, None], result, 0.0).astype(jnp.bfloat16)
    out_float = out_hidden.astype(jnp.float32)
    square_sum = jnp.sum(out_float * out_float, axis=(1, 2))
    slot_norm = jnp.sqrt(square_sum / (own_lengths.astype(jnp.float32) * width))
    picked = (positions[None, :] == own_lengths[:, None] - 1).astype(jnp.float32)
    last_rows = jnp.einsum("bs,bsd->bd", picked, out_float, precision=lax.Precision.HIGHEST)
    last_rounded = lax.optimization_barrier(rms_norm(last_rows, final_gain).astype(jnp.bfloat16))
    last_normed = last_rounded.astype(jnp.float32)
    every_last, every_norm = (
        lax.all_gather(last_normed, "req", axis=0, tiled=True),
        lax.all_gather(slot_norm, "req", axis=0, tiled=True),
    )
    logits = lax.dot_general(
        every_last.astype(jnp.bfloat16),
        vocab,
        (((1,), (1,)), ((), ())),
        preferred_element_type=jnp.float32,
    )
    slot_peak = lax.pmax(jnp.max(logits, axis=1), ("req", "mlp"))
    request_total = slot_request.shape[0]
    owners = slot_request[None, :] == jnp.arange(request_total, dtype=jnp.int32)[:, None]
    request_norm = jnp.sum(jnp.where(owners, every_norm[None, :], 0.0), axis=1)
    request_peak = jnp.sum(jnp.where(owners, slot_peak[None, :], 0.0), axis=1)
    return (out_hidden, request_norm, request_peak)


def solution(mesh):
    return jax.shard_map(
        per_device,
        mesh=mesh,
        in_specs=(
            P("req", None, None),
            P(),
            P(),
            P(),
            P(),
            P(),
            P(),
            P(),
            P(None, None, "mlp"),
            P("mlp", None),
            P("req", None, "mlp"),
            P("mlp", "req"),
            P("req", None, None),
            P("req", None, "mlp"),
            P(("req", "mlp"), None),
        ),
        out_specs=(P("req", None, None), P(), P()),
        check_vma=False,
    )
```

profile of v0, /device:TPU:0, one launch (start us, length us, event | category | flops | bytes accessed | tf_op | source)
XLA Modules:
  0.0 623.8 jit_solution(15625885839021791205)
XLA Ops:
  7.2 0.7 all-gather.8.cloned.1.call-update
  8.0 0.7 all-gather.6.cloned.1.call-update
  8.7 8.8 %copy.26 = bf16[2048,3,512]{0,2,1:T(8,128)(2,1)} copy(bf16[2048,3,512]{2,0,1:T(8,128)(2,1)} %param.27) | data formatting | bytes 12582912 | tf_op args[8]
  17.5 3.2 fusion.44
  20.8 0.2 copy-done.4
  21.0 9.1 %fusion.53 = f32[2,512,3,512]{1,3,2,0:T(8,128)S(1)} fusion(bf16[2048,3,512]{0,2,1:T(8,128)(2,1)} %copy.26, bf16[2,512,2048]{2,1,0:T(8,128)(2,1)S(1)} %copy-done.4, f32[2048]{0:T(1024)S(1)} %copy-done.13, f32[2,512]{1,0:T(2,128)S(1)} %add_rsqrt_fusion.1), kind=kOutput, calls=%fused_computation.55 | convolution fusion | flops 6450839552 | bytes 16789504 | tf_op jit(solution)/shard_map/dot_general | solution.py:62
  30.1 1.7 slice.51
  31.8 1.6 copy-done.9
  33.3 0.1 slice.74
  33.5 0.1 compare_select_fusion.1
  33.6 0.6 gather_fusion.2
  34.2 0.6 gather_fusion.3
  34.9 0.1 broadcast_add_fusion
  35.0 0.6 gather_fusion.4
  35.6 0.3 fusion.73
  36.0 19.5 %all-gather.8.cloned.1.call-done = bf16[64,16,512]{2,1,0:T(8,128)(2,1)} async-done(((bf16[2,16,512]{2,1,0:T(8,128)(2,1)}), bf16[64,16,512]{2,1,0:T(8,128)(2,1)}) %all-gather.8.cloned.1.call-update) | async-done | bytes 1048592 | tf_op jit(solution)/shard_map/all_gather | solution.py:69
  55.4 1.8 gather_fusion.1
  57.2 45.8 %all-gather.6.cloned.1.call-done = bf16[64,16,2048]{2,1,0:T(8,128)(2,1)} async-done(((bf16[2,16,2048]{2,1,0:T(8,128)(2,1)}), bf16[64,16,2048]{2,1,0:T(8,128)(2,1)}) %all-gather.6.cloned.1.call-update) | async-done | bytes 4194320 | tf_op jit(solution)/shard_map/all_gather | solution.py:68
  103.0 2.7 gather_fusion
  105.8 5.8 fusion.61
  111.6 2.9 subtract_convert_fusion
  114.4 1.5 pad_maximum_fusion
  116.0 28.0 %while.11 = (s32[]{:T(128)}, bf16[2,512,8,64]{1,3,2,0:T(8,128)(2,1)}, bf16[2,512,8,64]{1,3,2,0:T(8,128)(2,1)S(1)}, s32[2]{0:T(128)S(1)}, bf16[2,512,8,64]{1,3,2,...) while((s32[]{:T(128)}, bf16[2,512,8,64]{1,3,2,0:T(8,128)(2,1)}, ...), condition=%wide.region_4.6_spmd.clone, body=%wide.region_1.5_spmd.clone.sunk | while | flops 550241280 | bytes 19434588 | solution.py:104
  116.0 0.6 dynamic_slice.68
  116.6 0.6 iota_compare_fusion.5
  117.2 0.1 fusion.115
  117.3 7.6 %fusion.116 = (f32[8,512]{1,0:T(8,128)S(1)}, f32[8,512,512]{1,2,0:T(8,128)}) fusion(pred[512,512]{0,1:T(8,128)(4,1)S(1)} %fusion.115, bf16[2,512,8,64]{1,3,2,0:T(8,128)(2,1)} %get-tuple-element.155, s32[]{:T(128)} %get-tuple-element.143, bf16[2,512,8,64]{1,3,2,0:T(8,128)(2,1)} %get-tuple-element.154), kind=kOutput, calls=%fused_computation.116.clone.1 | convolution fusion | flops 276824576 | bytes 9716736 | tf_op jit(solution)/shard_map/while/body/eval_jaxpr/sub | solution.py:99
  124.9 5.0 fusion.117
  130.0 0.6 dynamic_slice.68
  130.5 0.6 iota_compare_fusion.5
  131.2 0.1 fusion.115
  131.3 7.6 %fusion.116 = (f32[8,512]{1,0:T(8,128)S(1)}, f32[8,512,512]{1,2,0:T(8,128)}) fusion(pred[512,512]{0,1:T(8,128)(4,1)S(1)} %fusion.115, bf16[2,512,8,64]{1,3,2,0:T(8,128)(2,1)} %get-tuple-element.155, s32[]{:T(128)} %get-tuple-element.143, bf16[2,512,8,64]{1,3,2,0:T(8,128)(2,1)} %get-tuple-element.154), kind=kOutput, calls=%fused_computation.116.clone.1 | convolution fusion | flops 276824576 | bytes 9716736 | tf_op jit(solution)/shard_map/while/body/eval_jaxpr/sub | solution.py:99
  138.9 5.0 fusion.117
  143.9 2.3 copy.27
  146.3 0.2 copy.32
  146.5 4.4 convolution_convert_fusion
  151.0 0.5 all-gather.10.cloned.1.call-update
  151.6 0.5 all-gather.12.cloned.1.call-update
  152.2 91.4 %all-reduce.4.cloned.1.call-done = bf16[2,512,2048]{2,1,0:T(8,128)(2,1)} async-done(((bf16[2,512,2048]{2,1,0:T(8,128)(2,1)}), bf16[2,512,2048]{2,1,0:T(8,128)(2,1)}) %all-reduce.4.cloned.1.call-update) | async-done | bytes 4194320 | tf_op jit(solution)/shard_map/psum | solution.py:108
  243.6 5.0 fusion.48
  248.7 0.9 copy-done.6
  249.5 3.6 fusion.50
  253.1 45.4 %all-gather.10.cloned.1.call-done = bf16[2048,2,1024]{2,1,0:T(2,128)(2,1)} async-done(((bf16[64,2,1024]{2,1,0:T(2,128)(2,1)}), bf16[2048,2,1024]{2,1,0:T(2,128)(2,1)}) %all-gather.10.cloned.1.call-update) | async-done | bytes 8388624 | tf_op jit(solution)/shard_map/all_gather | solution.py:117
  298.5 10.3 %copy.33 = bf16[256,8,2,1024]{3,1,2,0:T(8,128)(2,1)} copy(bf16[256,8,2,1024]{3,2,1,0:T(2,128)(2,1)} %bitcast.100) | data formatting | bytes 16777216
  308.8 13.3 %fusion.97 = f32[1024,2048]{1,0:T(8,128)} fusion(bf16[1024,2048]{1,0:T(8,128)(2,1)S(1)} %bitcast.102, bf16[2048,2048]{1,0:T(8,128)(2,1)} %bitcast.101), kind=kOutput, calls=%fused_computation.117 | convolution fusion | flops 8589934592 | bytes 20971520 | tf_op jit(solution)/shard_map/dot_general | solution.py:118
  322.0 24.4 %all-gather.12.cloned.1.call-done = bf16[1024,2048]{0,1:T(8,128)(2,1)} async-done(((bf16[1024,64]{0,1:T(8,128)(2,1)}), bf16[1024,2048]{0,1:T(8,128)(2,1)}) %all-gather.12.cloned.1.call-update) | async-done | bytes 4194320 | tf_op jit(solution)/shard_map/all_gather | solution.py:126
  346.4 11.2 %convolution_convert_fusion.1 = bf16[1024,2048]{1,0:T(8,128)(2,1)} fusion(bf16[1024,2048]{0,1:T(8,128)(2,1)} %all-gather.12.cloned.1.call-done, f32[1024,2048]{1,0:T(8,128)} %fusion.97), kind=kOutput, calls=%fused_computation.61 | convolution fusion | flops 4303355904 | bytes 16777216 | tf_op jit(solution)/shard_map/dot_general | solution.py:124
  357.7 0.6 copy-done.14
  358.3 0.6 dynamic-slice
  359.5 0.1 iota_compare_fusion.3
  359.6 0.1 compare_bitcast_fusion
  359.7 90.6 %all-reduce.6.cloned.1.call-done = bf16[2,512,2048]{2,1,0:T(8,128)(2,1)} async-done(((bf16[2,512,2048]{2,1,0:T(8,128)(2,1)}), bf16[2,512,2048]{2,1,0:T(8,128)(2,1)}) %all-reduce.6.cloned.1.call-update) | async-done | bytes 4194320 | tf_op jit(solution)/shard_map/psum | solution.py:129
  450.3 6.9 %multiply_reduce_fusion = (f32[2]{0:T(128)S(1)}, bf16[2,512,2048]{2,1,0:T(8,128)(2,1)S(1)}) fusion(bf16[2,512,2048]{2,1,0:T(8,128)(2,1)} %all-reduce.6.cloned.1.call-done, bf16[2,512,2048]{2,1,0:T(8,128)(2,1)} %all-reduce.4.cloned.1.call-done, bf16[2,512,2048]{2,1,0:T(8,128)(2,1)} %param.19, pred[2,512]{1,0:T(4,128)(4,1)S(1)} %iota_compare_fusion.3), kind=kLoop, calls=%fused_computation.54 | loop fusion | flops 25165822 | bytes 16778248 | tf_op jit(solution)/shard_map/reduce_sum | solution.py:134
  457.3 2.0 copy-done.7
  459.3 0.7 fusion.82
  459.9 0.1 fusion.78
  460.1 0.1 fusion.80
  460.2 24.8 %all-gather = bf16[32,2,2048]{2,1,0:T(2,128)(2,1)S(1)} all-gather(bf16[1,2,2048]{2,1,0:T(2,128)(2,1)S(1)} %bitcast.109), channel_id=1, replica_groups=mesh['req'=32,'mlp'=4] {'req'}, dimensions={0}, use_global_device_ids=true | all-gather | bytes 270336 | tf_op jit(solution)/shard_map/all_gather | solution.py:141
  484.9 0.1 reshape.230
  485.0 2.1 convolution_reduce_fusion
  487.2 64.5 %pmax.7 = f32[64]{0:T(128)S(1)} all-reduce(f32[64]{0:T(128)S(1)} %convolution_reduce_fusion), channel_id=1, replica_groups=mesh['req'=32,'mlp'=4] {'req','mlp'}, use_global_device_ids=true, to_apply=%region_12.14 | all-reduce | flops 64 | bytes 512 | tf_op jit(solution)/shard_map/pmax | solution.py:150
  551.6 0.1 sqrt_dynamic-update-slice_fusion
  551.7 64.6 %all-reduce = f32[64]{0:T(128)S(1)} all-reduce(f32[64]{0:T(128)S(1)} %sqrt_dynamic-update-slice_fusion), channel_id=1, replica_groups=mesh['req'=32,'mlp'=4] {'req'}, use_global_device_ids=true, to_apply=%add | all-reduce | flops 64 | bytes 512
  616.3 0.6 select_reduce_fusion
  (43 shorter events, 0.4 us)
Async XLA Ops:
  7.2 139.3 %copy-start = (bf16[512,2048]{1,0:T(8,128)(2,1)S(1)}, bf16[512,2048]{1,0:T(8,128)(2,1)}, u32[]{:S(2)}) copy-start(bf16[512,2048]{1,0:T(8,128)(2,1)} %param.28) | copy-start | bytes 6291460
  7.2 48.2 %all-gather.8.cloned.1.call-start = ((), (), s32[]{:S(2)}) async-start(), calls=%async_computation.1 | async-start | bytes 1081344 | tf_op jit(solution)/shard_map/all_gather | solution.py:69
  7.9 95.1 %all-gather.6.cloned.1.call-start = ((), (), s32[]{:S(2)}) async-start(), calls=%async_computation | async-start | bytes 4325376 | tf_op jit(solution)/shard_map/all_gather | solution.py:68
  8.7 234.9 %all-reduce.4.cloned.1.call-start = ((), (), s32[]{:S(2)}) async-start(), calls=%async_computation.2 | async-start | bytes 8388608 | tf_op jit(solution)/shard_map/psum | solution.py:108
  17.5 3.4 copy-start.4
  17.5 3.4 copy-start.13
  30.1 3.3 copy-start.9
  30.1 3.4 copy-start.12
  30.1 3.5 copy-start.1
  30.1 4.1 copy-start.2
  30.1 4.9 copy-start.3
  150.9 147.5 %all-gather.10.cloned.1.call-start = ((), (), s32[]{:S(2)}) async-start(), calls=%async_computation.3 | async-start | bytes 8650752 | tf_op jit(solution)/shard_map/all_gather | solution.py:117
  151.5 194.9 %all-gather.12.cloned.1.call-start = ((), (), s32[]{:S(2)}) async-start(), calls=%async_computation.4 | async-start | bytes 4325376 | tf_op jit(solution)/shard_map/all_gather | solution.py:126
  152.1 96.5 %copy-start.10 = (f32[2048]{0:T(1024)S(1)}, f32[2048]{0:T(1024)}, u32[]{:S(2)}) copy-start(f32[2048]{0:T(1024)} %param.25) | copy-start | bytes 24580
  152.1 298.2 %all-reduce.6.cloned.1.call-start = ((), (), s32[]{:S(2)}) async-start(), calls=%async_computation.5 | async-start | bytes 8388608 | tf_op jit(solution)/shard_map/psum | solution.py:129
  243.6 5.1 copy-start.5
  243.6 5.9 copy-start.6
  298.5 10.3 %copy-start.8 = (bf16[2,512,2048]{2,1,0:T(8,128)(2,1)S(1)}, bf16[2,512,2048]{2,1,0:T(8,128)(2,1)}, u32[]{:S(2)}) copy-start(bf16[2,512,2048]{2,1,0:T(8,128)(2,1)} %fusion.50) | copy-start | bytes 12582916
  357.6 0.7 copy-start.14
  457.3 2.0 copy-start.7
  457.3 2.8 copy-start.11
Sparse Core Ops, SparseCore 0:
  10.3 45.0 all-gather.7
  57.7 45.2 all-gather.5
  151.1 92.4 all-reduce.3
  246.0 52.4 all-gather.9
  300.8 45.5 all-gather.11
  357.8 92.4 all-reduce.5
where the time goes:
time: 624 us
  waiting for transfers between devices  320 us (51%)
  blocking collectives  154 us (25%)
  matrix products  71.7 us (11%)
  local copies, waits for them, and re-layouts  37.1 us (6%)
  other arithmetic  26.4 us (4%)
  between operations  15 us (2%)
    psum x1, waiting for transfers between devices, per_device(): lax.psum(head_part.astype(jnp.bfloat16), 'mlp').astype(jnp.float32)  91.4 us
    psum x1, waiting for transfers between devices, per_device(): lax.psum(unit_part.astype(jnp.bfloat16), 'mlp').astype(jnp.float32)  90.6 us
    unnamed x1, blocking collectives  64.6 us
    pmax x1, blocking collectives, per_device(): slot_peak = lax.pmax(jnp.max(logits, axis=1), ('req', 'mlp'))  64.5 us
    all_gather x1, waiting for transfers between devices, per_device(): lax.all_gather(adapter_down, 'req', axis=0, tiled=True)  45.8 us
    all_gather x1, waiting for transfers between devices, per_device(): shard_piece = lax.all_gather(w_gateup, 'req', axis=0, tiled=True)  45.4 us
    unnamed x35, local copies, waits for them, and re-layouts  25.3 us
    all_gather x1, blocking collectives, per_device(): lax.all_gather(last_normed, 'req', axis=0, tiled=True)  24.8 us
  transfers between devices with their start and end apart: 6, of which 6 were waited for; matrix products, arithmetic and copies ran while one was open for 10% of the time, Pallas kernels for 0%

commit v1 on v0

--- a/solution.py
+++ b/solution.py
@@ -105,7 +105,9 @@
     head_part = jnp.dot(
         attended.reshape(row_count, head_cols), w_out, preferred_element_type=jnp.float32
     )
-    mixed_heads = lax.psum(head_part.astype(jnp.bfloat16), "mlp").astype(jnp.float32)
+    mixed_heads = jnp.sum(lax.all_gather(head_part.astype(jnp.bfloat16), "mlp"), axis=0).astype(
+        jnp.float32
+    )
     stream = (residual_in + mixed_heads.reshape(slots_number, sequence_length, width)).astype(
         jnp.bfloat16
     )

time: 624 us -> 647 us (1.037); the launches traced: 624 us -> 639 us
  other arithmetic: 26.4 us -> 38.1 us
    all_gather x0 -> x1, waiting for transfers between devices: none -> 146 us  [per_device(): lax.all_gather(head_part.astype(jnp.bfloat16), 'mlp')]
    psum x1 -> x0, waiting for transfers between devices: 91.4 us -> none  [per_device(): lax.psum(head_part.astype(jnp.bfloat16), 'mlp').astype(jnp.float32)]
    all_gather x1, waiting for transfers between devices: 45.4 us -> 5.25 us  [per_device(): shard_piece = lax.all_gather(w_gateup, 'req', axis=0, tiled=True)]
    reduce_sum x0 -> x1, other arithmetic: none -> 12.3 us  [per_device(): jnp.sum(lax.all_gather(head_part.astype(jnp.bfloat16), 'mlp'), axis=0)]
    all_gather x1, waiting for transfers between devices: 24.4 us -> 16.4 us  [per_device(): lax.all_gather(w_down, 'req', axis=1, tiled=True)]
    unnamed x35 -> x37, local copies, waits for them, and re-layouts: 25.3 us -> 24.3 us
  transfers between devices with their start and end apart: 6 -> 6, of which waited for: 6 -> 6; matrix products, arithmetic and copies ran while one was open for 10% -> 18% of each run, Pallas kernels for 0% -> 0%
where the time goes in v1:
time: 647 us; the launch traced here: 639 us
  waiting for transfers between devices  325 us (50%)
  blocking collectives  154 us (24%)
  matrix products  69.6 us (11%)
  other arithmetic  38.1 us (6%)
  local copies, waits for them, and re-layouts  36.1 us (6%)
  between operations  15.2 us (2%)
    all_gather x1, waiting for transfers between devices, per_device(): lax.all_gather(head_part.astype(jnp.bfloat16), 'mlp')  146 us
    psum x1, waiting for transfers between devices, per_device(): lax.psum(unit_part.astype(jnp.bfloat16), 'mlp').astype(jnp.float32)  90.7 us
    unnamed x1, blocking collectives  64.6 us
    pmax x1, blocking collectives, per_device(): slot_peak = lax.pmax(jnp.max(logits, axis=1), ('req', 'mlp'))  64.5 us
    all_gather x1, waiting for transfers between devices, per_device(): lax.all_gather(adapter_down, 'req', axis=0, tiled=True)  45.8 us
    all_gather x1, blocking collectives, per_device(): lax.all_gather(last_normed, 'req', axis=0, tiled=True)  24.8 us
    unnamed x37, local copies, waits for them, and re-layouts  24.3 us
    all_gather x1, waiting for transfers between devices, per_device(): lax.all_gather(adapter_up, 'req', axis=0, tiled=True)  18.7 us
  transfers between devices with their start and end apart: 6, of which 6 were waited for; matrix products, arithmetic and copies ran while one was open for 18% of the time, Pallas kernels for 0%

profile of v1, /device:TPU:0, one launch (start us, length us, event | category | flops | bytes accessed | tf_op | source)
XLA Modules:
  0.0 638.8 jit_solution(17526789442634656808)
XLA Ops:
  7.2 0.7 all-gather.10.cloned.1.call-update
  8.0 0.7 all-gather.8.cloned.1.call-update
  8.7 0.7 all-gather.12.cloned.1.call-update
  9.4 8.8 %copy.26 = bf16[2048,3,512]{0,2,1:T(8,128)(2,1)} copy(bf16[2048,3,512]{2,0,1:T(8,128)(2,1)} %param.27) | data formatting | bytes 12582912 | tf_op args[8]
  18.3 3.2 fusion.44
  21.5 0.2 copy-done.5
  21.7 9.1 %fusion.53 = f32[2,512,3,512]{1,3,2,0:T(8,128)S(1)} fusion(bf16[2048,3,512]{0,2,1:T(8,128)(2,1)} %copy.26, bf16[2,512,2048]{2,1,0:T(8,128)(2,1)S(1)} %copy-done.5, f32[2048]{0:T(1024)S(1)} %copy-done.14, f32[2,512]{1,0:T(2,128)S(1)} %add_rsqrt_fusion.1), kind=kOutput, calls=%fused_computation.55 | convolution fusion | flops 6450839552 | bytes 16789504 | tf_op jit(solution)/shard_map/dot_general | solution.py:62
  30.9 1.7 slice.51
  32.6 1.5 copy-done.10
  34.1 0.1 slice.74
  34.3 0.1 compare_select_fusion.1
  34.4 0.6 gather_fusion.2
  35.0 0.6 gather_fusion.3
  35.6 0.1 broadcast_add_fusion
  35.7 0.6 gather_fusion.4
  36.4 0.3 fusion.73
  36.7 18.7 %all-gather.10.cloned.1.call-done = bf16[64,16,512]{2,1,0:T(8,128)(2,1)} async-done(((bf16[2,16,512]{2,1,0:T(8,128)(2,1)}), bf16[64,16,512]{2,1,0:T(8,128)(2,1)}) %all-gather.10.cloned.1.call-update) | async-done | bytes 1048592 | tf_op jit(solution)/shard_map/all_gather | solution.py:69
  55.4 1.8 gather_fusion.1
  57.2 45.8 %all-gather.8.cloned.1.call-done = bf16[64,16,2048]{2,1,0:T(8,128)(2,1)} async-done(((bf16[2,16,2048]{2,1,0:T(8,128)(2,1)}), bf16[64,16,2048]{2,1,0:T(8,128)(2,1)}) %all-gather.8.cloned.1.call-update) | async-done | bytes 4194320 | tf_op jit(solution)/shard_map/all_gather | solution.py:68
  103.0 2.7 gather_fusion
  105.8 5.8 fusion.61
  111.6 2.9 subtract_convert_fusion
  114.4 1.5 pad_maximum_fusion
  116.0 28.6 %while.11 = (s32[]{:T(128)}, bf16[2,512,8,64]{1,3,2,0:T(8,128)(2,1)}, bf16[2,512,8,64]{1,3,2,0:T(8,128)(2,1)S(1)}, s32[2]{0:T(128)S(1)}, bf16[2,512,8,64]{1,3,2,...) while((s32[]{:T(128)}, bf16[2,512,8,64]{1,3,2,0:T(8,128)(2,1)}, ...), condition=%wide.region_4.6_spmd.clone, body=%wide.region_1.5_spmd.clone.sunk | while | flops 550241280 | bytes 19434588 | solution.py:104
  116.0 0.6 dynamic_slice.68
  116.6 0.6 iota_compare_fusion.5
  117.2 0.1 fusion.114
  117.3 7.6 %fusion.115 = (f32[8,512]{1,0:T(8,128)S(1)}, f32[8,512,512]{1,2,0:T(8,128)}) fusion(pred[512,512]{0,1:T(8,128)(4,1)S(1)} %fusion.114, bf16[2,512,8,64]{1,3,2,0:T(8,128)(2,1)} %get-tuple-element.153, s32[]{:T(128)} %get-tuple-element.141, bf16[2,512,8,64]{1,3,2,0:T(8,128)(2,1)} %get-tuple-element.152), kind=kOutput, calls=%fused_computation.116.clone.1 | convolution fusion | flops 276824576 | bytes 9716736 | tf_op jit(solution)/shard_map/while/body/eval_jaxpr/sub | solution.py:99
  124.9 5.1 fusion.116
  130.0 0.6 dynamic_slice.68
  130.6 0.6 iota_compare_fusion.5
  131.2 0.1 fusion.114
  131.4 7.6 %fusion.115 = (f32[8,512]{1,0:T(8,128)S(1)}, f32[8,512,512]{1,2,0:T(8,128)}) fusion(pred[512,512]{0,1:T(8,128)(4,1)S(1)} %fusion.114, bf16[2,512,8,64]{1,3,2,0:T(8,128)(2,1)} %get-tuple-element.153, s32[]{:T(128)} %get-tuple-element.141, bf16[2,512,8,64]{1,3,2,0:T(8,128)(2,1)} %get-tuple-element.152), kind=kOutput, calls=%fused_computation.116.clone.1 | convolution fusion | flops 276824576 | bytes 9716736 | tf_op jit(solution)/shard_map/while/body/eval_jaxpr/sub | solution.py:99
  139.0 5.2 fusion.116
  144.6 2.3 copy.27
  146.9 0.2 copy.32
  147.2 4.4 convolution_convert_fusion
  151.6 0.5 all-gather.14.cloned.1.call-update
  152.2 5.3 all-gather.12.cloned.1.call-done
  157.5 10.1 %copy.33 = bf16[256,8,2,1024]{3,1,2,0:T(8,128)(2,1)} copy(bf16[256,8,2,1024]{3,2,1,0:T(2,128)(2,1)} %bitcast.106) | data formatting | bytes 16777216
  167.6 145.8 %all-gather.16.cloned.1.call-done = bf16[4096,2048]{1,0:T(8,128)(2,1)} async-done(((bf16[1024,2048]{1,0:T(8,128)(2,1)}), bf16[4096,2048]{1,0:T(8,128)(2,1)}) %all-gather.16.cloned.1.call-update) | async-done | bytes 16777232 | tf_op jit(solution)/shard_map/all_gather | solution.py:108
  313.4 12.3 %reduce_sum.76 = bf16[1024,2048]{1,0:T(8,128)(2,1)} reduce(bf16[4,1024,2048]{2,1,0:T(8,128)(2,1)} %bitcast.104, bf16[]{:T(256)} %constant.60.clone.1), dimensions={0}, to_apply=%region_5.7 | reduce | flops 6291456 | bytes 20971522 | tf_op jit(solution)/shard_map/reduce_sum | solution.py:108
  325.7 5.1 fusion.48
  330.8 0.9 copy-done.7
  331.7 2.4 fusion.50
  334.1 1.0 copy-done.9
  335.1 11.0 %fusion.96 = f32[1024,2048]{1,0:T(8,128)} fusion(bf16[1024,2048]{1,0:T(8,128)(2,1)S(1)} %bitcast.108, bf16[2048,2048]{1,0:T(8,128)(2,1)S(1)} %bitcast.107), kind=kOutput, calls=%fused_computation.117 | convolution fusion | flops 8589934592 | bytes 20971520 | tf_op jit(solution)/shard_map/dot_general | solution.py:120
  346.1 16.4 %all-gather.14.cloned.1.call-done = bf16[1024,2048]{0,1:T(8,128)(2,1)} async-done(((bf16[1024,64]{0,1:T(8,128)(2,1)}), bf16[1024,2048]{0,1:T(8,128)(2,1)}) %all-gather.14.cloned.1.call-update) | async-done | bytes 4194320 | tf_op jit(solution)/shard_map/all_gather | solution.py:128
  362.5 11.1 %convolution_convert_fusion.1 = bf16[1024,2048]{1,0:T(8,128)(2,1)} fusion(bf16[1024,2048]{0,1:T(8,128)(2,1)} %all-gather.14.cloned.1.call-done, f32[1024,2048]{1,0:T(8,128)} %fusion.96), kind=kOutput, calls=%fused_computation.61 | convolution fusion | flops 4303355904 | bytes 16777216 | tf_op jit(solution)/shard_map/dot_general | solution.py:126
  373.6 0.6 copy-done.15
  374.3 0.6 dynamic-slice
  375.6 90.7 %all-reduce.3.cloned.1.call-done = bf16[2,512,2048]{2,1,0:T(8,128)(2,1)} async-done(((bf16[2,512,2048]{2,1,0:T(8,128)(2,1)}), bf16[2,512,2048]{2,1,0:T(8,128)(2,1)}) %all-reduce.3.cloned.1.call-update) | async-done | bytes 4194320 | tf_op jit(solution)/shard_map/psum | solution.py:131
  466.3 6.3 fusion.52
  472.6 1.2 multiply_reduce_fusion
  473.8 0.7 fusion.82
  474.5 0.2 copy-done.8
  474.7 0.1 fusion.78
  475.0 24.8 %all-gather.1 = bf16[32,2,2048]{2,1,0:T(2,128)(2,1)S(1)} all-gather(bf16[1,2,2048]{2,1,0:T(2,128)(2,1)S(1)} %bitcast.114), channel_id=1, replica_groups=mesh['req'=32,'mlp'=4] {'req'}, dimensions={0}, use_global_device_ids=true | all-gather | bytes 270336 | tf_op jit(solution)/shard_map/all_gather | solution.py:143
  499.7 0.1 reshape.228
  499.8 2.1 convolution_reduce_fusion
  502.0 64.5 %pmax.7 = f32[64]{0:T(128)S(1)} all-reduce(f32[64]{0:T(128)S(1)} %convolution_reduce_fusion), channel_id=1, replica_groups=mesh['req'=32,'mlp'=4] {'req','mlp'}, use_global_device_ids=true, to_apply=%region_12.14 | all-reduce | flops 64 | bytes 512 | tf_op jit(solution)/shard_map/pmax | solution.py:152
  566.4 0.1 sqrt_dynamic-update-slice_fusion
  566.5 64.6 %all-reduce = f32[64]{0:T(128)S(1)} all-reduce(f32[64]{0:T(128)S(1)} %sqrt_dynamic-update-slice_fusion), channel_id=1, replica_groups=mesh['req'=32,'mlp'=4] {'req'}, use_global_device_ids=true, to_apply=%add | all-reduce | flops 64 | bytes 512
  631.1 0.6 select_reduce_fusion
  (47 shorter events, 0.6 us)
Async XLA Ops:
  7.2 140.0 %copy-start = (bf16[512,2048]{1,0:T(8,128)(2,1)S(1)}, bf16[512,2048]{1,0:T(8,128)(2,1)}, u32[]{:S(2)}) copy-start(bf16[512,2048]{1,0:T(8,128)(2,1)} %param.28) | copy-start | bytes 6291460
  7.2 48.2 %all-gather.10.cloned.1.call-start = ((), (), s32[]{:S(2)}) async-start(), calls=%async_computation.1 | async-start | bytes 1081344 | tf_op jit(solution)/shard_map/all_gather | solution.py:69
  7.9 95.1 %all-gather.8.cloned.1.call-start = ((), (), s32[]{:S(2)}) async-start(), calls=%async_computation | async-start | bytes 4325376 | tf_op jit(solution)/shard_map/all_gather | solution.py:68
  8.7 148.8 %all-gather.12.cloned.1.call-start = ((), (), s32[]{:S(2)}) async-start(), calls=%async_computation.2 | async-start | bytes 8650752 | tf_op jit(solution)/shard_map/all_gather | solution.py:119
  9.4 304.0 %all-gather.16.cloned.1.call-start = ((), (), s32[]{:S(2)}) async-start(), calls=%async_computation.5 | async-start | bytes 20971520 | tf_op jit(solution)/shard_map/all_gather | solution.py:108
  18.3 3.4 copy-start.5
  18.3 3.4 copy-start.14
  30.8 3.3 copy-start.10
  30.8 3.4 copy-start.13
  30.8 3.5 copy-start.2
  30.8 4.2 copy-start.3
  30.8 4.9 copy-start.4
  151.6 210.9 %all-gather.14.cloned.1.call-start = ((), (), s32[]{:S(2)}) async-start(), calls=%async_computation.3 | async-start | bytes 4325376 | tf_op jit(solution)/shard_map/all_gather | solution.py:128
  152.2 314.1 %all-reduce.3.cloned.1.call-start = ((), (), s32[]{:S(2)}) async-start(), calls=%async_computation.4 | async-start | bytes 8388608 | tf_op jit(solution)/shard_map/psum | solution.py:131
  325.7 5.1 copy-start.6
  325.7 6.0 copy-start.7
  325.7 6.0 copy-start.11
  331.7 3.4 copy-start.9
  373.6 0.7 copy-start.15
  472.6 2.1 copy-start.8
  472.6 2.3 copy-start.12
  472.6 159.1 %copy-start.1 = (bf16[512,2048]{1,0:T(8,128)(2,1)S(1)}, bf16[512,2048]{1,0:T(8,128)(2,1)}, u32[]{:S(2)}) copy-start(bf16[512,2048]{1,0:T(8,128)(2,1)} %param.28) | copy-start | bytes 6291460
Sparse Core Ops, SparseCore 0:
  10.3 45.0 all-gather.9
  57.7 45.2 all-gather.7
  105.3 52.1 all-gather.11
  159.6 153.7 all-gather.15
  315.5 46.8 all-gather.13
  373.8 92.4 all-reduce.2
